TPU v7x, 256 devices: a whole 4x4x8 slice. The times are simulated.
256 devices in a mesh: dp: 32 (over y, x, core), tensor: 8 (over z).
Axes of the slice: x: 4, y: 4, z: 8, core: 2. Of those that a mesh axis runs over, the one named last changes fastest.
Arguments:
- rank_query: bfloat16 [256, 32, 5120], P('dp', None, 'tensor'), may hold values from -4.5 to 4.5
- rank_key: bfloat16 [256, 32, 5120], P('dp', None, 'tensor'), may hold values from -4.5 to 4.5
- rank_value: bfloat16 [256, 32, 5120], P('dp', None, 'tensor'), may hold values from -6 to 6
- rank_resid: bfloat16 [256, 32, 5120], P(('dp', 'tensor')), may hold values from -4 to 4
- out_weight: bfloat16 [5120, 5120], P('tensor', 'dp'), may hold values from -0.25 to 0.25
- rank_gain: bfloat16 [5120], replicated, may hold values from 0.099609375 to 1.8984375
- score_weight: bfloat16 [5120], replicated, may hold values from -0.078125 to 0.078125
- pair_index: int32 [256, 3], P(('dp', 'tensor')), may hold values from 0 to 31, as said below
- cand_rank: int32 [1024, 8], P('dp'), may hold values from 0 to 7, each once within a row
- cand_len: int32 [1024, 8], P('dp'), may hold values from 1 to 8, 39 in all within a row
- blend_owner: int32 [32, 32], P('dp'), may hold values from 0 to 31, each once within a row
- blend_rows: bfloat16 [1024, 8, 8, 4096], P('dp', None, None, 'tensor'), may hold values from -6 to 6
- blend_gain: bfloat16 [4096], replicated, may hold values from 0.099609375 to 1.8984375
- blend_weight: bfloat16 [4096, 3, 2048], P('dp', None, 'tensor'), may hold values from -0.09375 to 0.09375
Outputs:
- rank_hidden: bfloat16 [256, 32, 5120], P(('dp', 'tensor'))
- cand_score: float32 [1024, 8], P('dp')
- blended_qkv: bfloat16 [1024, 24, 3, 2048], P('dp', None, None, 'tensor')
Inputs may be any that keep to these rules, and one draw needn't show every extreme that they name: `pair_index`: column 0 is a prompt of the pair's own group of 32 prompts (pair p belongs to group p // 8); columns 1 and 2 are two different candidates of that prompt. `cand_rank`: each row gives every rank once. `blend_owner`: each row names every group once.
All inputs are finite; a program needn't handle non-finite values.
Results may differ from a plain program's by a relative error of at most 0.024.
Values may be sent and summed in bfloat16 or wider, within the bound.
No kernel may reach another device: no remote copies, remote signals or barrier semaphores. Data moves between devices by JAX's collectives and lax.ppermute only.
A program may use at most 128 MiB of HBM per device.

v0:
```python
import math
import jax
import jax.numpy as jnp
from jax import lax
from jax.sharding import PartitionSpec as P

HR = 40
HDR = 128


def pair_attention(queries, keys_in, values_in, head_count):
    pair_count, length, row_width = queries.shape
    head_size = row_width // head_count
    query_heads = queries.reshape(pair_count, length, head_count, head_size)
    key_heads = keys_in.reshape(pair_count, length, head_count, head_size)
    value_heads = values_in.reshape(pair_count, length, head_count, head_size)
    scores = jnp.einsum(
        "pihd,pjhd->phij", query_heads, key_heads, preferred_element_type=jnp.float32
    ) * (1.0 / math.sqrt(HDR))
    highest = jnp.max(scores, axis=-1, keepdims=True)
    weights = jnp.exp(scores - highest)
    soft_weights = (weights / jnp.sum(weights, axis=-1, keepdims=True)).astype(jnp.bfloat16)
    context = jnp.einsum(
        "phij,pjhd->pihd", soft_weights, value_heads, preferred_element_type=jnp.float32
    )
    return context.astype(jnp.bfloat16).reshape(pair_count * length, row_width)


def encode(rows_in, blend_gain, blend_weight):
    whole_rows = lax.all_gather(rows_in, "tensor", axis=3, tiled=True)
    prompts, pick_count, length, features = whole_rows.shape
    flat_rows = whole_rows.reshape(prompts * pick_count * length, features)
    as_float = flat_rows.astype(jnp.float32)
    scale_rows = lax.rsqrt(jnp.mean(as_float * as_float, axis=-1, keepdims=True) + 1e-06)
    blend_normed = (as_float * scale_rows * blend_gain.astype(jnp.float32)).astype(jnp.bfloat16)
    columns = blend_weight.shape[1] * blend_weight.shape[2]
    portion = lax.all_gather(blend_weight, "dp", axis=0, tiled=True)
    projected = jnp.dot(
        blend_normed, portion.reshape(portion.shape[0], columns), preferred_element_type=jnp.float32
    )
    return projected.astype(jnp.bfloat16).reshape(
        prompts, pick_count * length, blend_weight.shape[1], blend_weight.shape[2]
    )


def body(
    rank_query,
    rank_key,
    rank_value,
    rank_resid,
    out_weight,
    rank_gain,
    score_weight,
    pair_index,
    cand_rank,
    cand_len,
    blend_owner,
    blend_rows,
    blend_gain,
    blend_weight,
):
    tensor_count = lax.axis_size("tensor")
    local_heads = HR // tensor_count
    length = rank_query.shape[1]
    context = pair_attention(rank_query, rank_key, rank_value, local_heads)
    own_pairs = rank_resid.shape[0]
    own_rows = own_pairs * length
    term_rows = jnp.dot(
        context,
        lax.all_gather(out_weight, "dp", axis=1, tiled=True),
        preferred_element_type=jnp.float32,
    )
    summed = lax.psum(term_rows.astype(jnp.bfloat16), "tensor").astype(jnp.float32)
    part_sum = lax.dynamic_slice_in_dim(summed, lax.axis_index("tensor") * own_rows, own_rows, 0)
    mixed_rows = rank_resid.reshape(own_rows, -1).astype(jnp.float32) + part_sum
    mean_square = jnp.mean(mixed_rows * mixed_rows, axis=-1, keepdims=True)
    normed = mixed_rows * lax.rsqrt(mean_square + 1e-05) * rank_gain.astype(jnp.float32)
    rank_hidden = normed.astype(jnp.bfloat16).reshape(rank_resid.shape)
    leading = normed.reshape(own_pairs, length, -1)[:, 0, :]
    pair_logit = jnp.sum(leading * score_weight.astype(jnp.float32), axis=-1)
    prompt_count = cand_rank.shape[0]
    cand_count = cand_rank.shape[1]
    slot_ids = jnp.arange(prompt_count * cand_count, dtype=jnp.int32)
    base_slot = pair_index[:, 0] * cand_count
    upward = jnp.where(
        (base_slot + pair_index[:, 1])[:, None] == slot_ids[None, :], pair_logit[:, None], 0.0
    )
    downward = jnp.where(
        (base_slot + pair_index[:, 2])[:, None] == slot_ids[None, :], pair_logit[:, None], 0.0
    )
    vote_sums = jnp.sum(upward - downward, axis=0).reshape(prompt_count, cand_count)
    cand_score = lax.psum(vote_sums, "tensor")
    places = jnp.arange(3, dtype=jnp.int32)
    matched = cand_rank[:, None, :] == places[None, :, None]
    labels = jnp.arange(cand_count, dtype=jnp.int32)
    chosen = jnp.sum(jnp.where(matched, labels[None, None, :], 0), axis=-1)
    chosen_len = jnp.sum(jnp.where(matched, cand_len[:, None, :], 0), axis=-1)
    prompt_ids = jnp.arange(prompt_count, dtype=jnp.int32)
    picked = blend_rows[prompt_ids[:, None], chosen]
    positions = jnp.arange(blend_rows.shape[2], dtype=jnp.int32)
    live_rows = positions[None, None, :] < chosen_len[:, :, None]
    picked = jnp.where(live_rows[..., None], picked, jnp.zeros((), jnp.bfloat16))
    owners = blend_owner[0]
    sender = jnp.sum(
        jnp.where(owners[None, :] == prompt_ids[:, None], prompt_ids[None, :], 0), axis=1
    )
    outgoing = picked[sender]
    arrived = lax.all_to_all(outgoing, "dp", split_axis=0, concat_axis=0, tiled=True)
    blended_qkv = encode(arrived, blend_gain, blend_weight)
    return (rank_hidden, cand_score, blended_qkv)


def solution(mesh):
    placed = (
        P("dp", None, "tensor"),
        P("dp", None, "tensor"),
        P("dp", None, "tensor"),
        P(("dp", "tensor"), None, None),
        P("tensor", "dp"),
        P(),
        P(),
        P(("dp", "tensor"), None),
        P("dp", None),
        P("dp", None),
        P("dp", None),
        P("dp", None, None, "tensor"),
        P(),
        P("dp", None, "tensor"),
    )
    return jax.shard_map(
        body,
        mesh=mesh,
        in_specs=placed,
        out_specs=(P(("dp", "tensor"), None, None), P("dp", None), P("dp", None, None, "tensor")),
        check_vma=False,
    )
```

profile of v0, /device:TPU:2, one launch (start us, length us, event | category | flops | bytes accessed | tf_op | source)
XLA Modules:
  0.0 343.9 jit_solution(1360914309973684097)
XLA Ops:
  7.2 0.9 select_reduce_fusion.2
  8.2 0.1 reshape.142
  8.4 0.1 iota_compare_fusion
  8.5 0.8 select_reduce_fusion
  9.3 0.6 pad_clamp_fusion
  9.9 2.0 gather_fusion
  11.9 1.3 broadcast_select_fusion
  13.3 1.7 gather_fusion.1
  15.0 21.0 %all_to_all.5 = bf16[32,3,8,512]{3,2,1,0:T(8,128)(2,1)} all-to-all(bf16[32,3,8,512]{3,2,1,0:T(8,128)(2,1)} %gather_fusion.1), channel_id=1, replica_groups=mesh['dp'=32,'tensor'=8] {'dp'}, dimensions={0} | all-to-all | bytes 1572864 | tf_op jit(solution)/shard_map/all_to_all | solution.py:108
  36.1 0.7 all-gather.4.cloned.1.call-update
  36.9 1.7 copy.63
  38.7 1.0 fusion.32
  39.7 0.3 convolution_multiply_fusion
  40.0 1.3 fusion.6
  41.3 0.2 copy.58
  41.5 0.6 fusion.31
  44.0 0.7 convert_element_type.58
  44.7 66.2 %all-gather.6.cloned.1.call-done = bf16[32,3,8,4096]{3,2,1,0:T(8,128)(2,1)} async-done(((bf16[32,3,8,512]{3,2,1,0:T(8,128)(2,1)}), bf16[32,3,8,4096]{3,2,1,0:T(8,128)(2,1)}) %all-gather.6.cloned.1.call-update) | async-done | bytes 6291472 | tf_op jit(solution)/shard_map/all_gather | solution.py:30
  110.9 4.1 %fusion.1 = f32[32,3,8]{2,1,0:T(4,128)S(1)} fusion(bf16[32,3,8,4096]{3,2,1,0:T(8,128)(2,1)} %all-gather.6.cloned.1.call-done), kind=kLoop, calls=%fused_computation.5 | loop fusion | flops 9436416 | bytes 6294528 | tf_op jit(solution)/shard_map/reduce_sum | solution.py:34
  115.2 50.6 %all-gather.4.cloned.1.call-done = bf16[640,5120]{0,1:T(8,128)(2,1)} async-done(((bf16[640,160]{0,1:T(8,128)(2,1)}), bf16[640,5120]{0,1:T(8,128)(2,1)}) %all-gather.4.cloned.1.call-update) | async-done | bytes 6553616 | tf_op jit(solution)/shard_map/all_gather | solution.py:70
  165.7 6.6 %convolution_convert_fusion = bf16[256,5120]{1,0:T(8,128)(2,1)} fusion(bf16[640,5120]{0,1:T(8,128)(2,1)} %all-gather.4.cloned.1.call-done, bf16[32,8,5,128]{3,2,1,0:T(8,128)(2,1)S(1)} %bitcast.74), kind=kOutput, calls=%fused_computation.8 | convolution fusion | flops 1679032320 | bytes 9502720 | tf_op jit(solution)/shard_map/dot_general | solution.py:68
  172.4 8.2 %fusion.3 = bf16[32,3,8,4096]{3,2,1,0:T(8,128)(2,1)} fusion(bf16[32,3,8,4096]{3,2,1,0:T(8,128)(2,1)} %all-gather.6.cloned.1.call-done, f32[4096]{0:T(1024)S(1)} %convert_element_type.58, f32[32,3,8]{2,1,0:T(4,128)S(1)} %copy.62), kind=kLoop, calls=%fused_computation.7 | loop fusion | flops 12582912 | bytes 12602368 | tf_op jit(solution)/shard_map/convert_element_type | solution.py:35
  180.5 47.1 %all-gather.8.cloned.1.call-done = bf16[4096,3,256]{0,2,1:T(8,128)(2,1)} async-done(((bf16[128,3,256]{0,2,1:T(8,128)(2,1)}), bf16[4096,3,256]{0,2,1:T(8,128)(2,1)}) %all-gather.8.cloned.1.call-update) | async-done | bytes 6291472 | tf_op jit(solution)/shard_map/all_gather | solution.py:37
  227.7 9.9 %convolution_convert_fusion.1 = bf16[768,768]{1,0:T(8,128)(2,1)} fusion(bf16[768,4096]{1,0:T(8,128)(2,1)} %bitcast.72, bf16[4096,768]{0,1:T(8,128)(2,1)} %bitcast.76), kind=kOutput, calls=%fused_computation.9 | convolution fusion | flops 4832428032 | bytes 13762560 | tf_op jit(solution)/shard_map/dot_general | solution.py:38
  237.6 3.7 %reshape.140 = bf16[32,24,3,256]{3,2,1,0:T(4,128)(2,1)} reshape(bf16[768,768]{1,0:T(8,128)(2,1)} %convolution_convert_fusion.1) | data formatting | bytes 2359296 | tf_op jit(solution)/shard_map/reshape | solution.py:41
  241.3 2.6 copy.64
  243.9 72.1 %all-reduce.2.cloned.1.call-done = bf16[256,5120]{1,0:T(8,128)(2,1)} async-done(((bf16[256,5120]{1,0:T(8,128)(2,1)}), bf16[256,5120]{1,0:T(8,128)(2,1)}) %all-reduce.2.cloned.1.call-update) | async-done | bytes 2621456 | tf_op jit(solution)/shard_map/psum | solution.py:73
  316.0 1.2 multiply_reduce_fusion
  317.2 1.8 fusion.7
  319.1 0.6 multiply_reduce_fusion.1
  319.7 0.6 select_subtract_fusion
  320.2 17.1 %psum.15 = f32[32,8]{0,1:T(8,128)} all-reduce(f32[32,8]{0,1:T(8,128)S(1)} %select_subtract_fusion), channel_id=1, replica_groups=mesh['dp'=32,'tensor'=8] {'tensor'}, use_global_device_ids=true, to_apply=%region_5.6 | all-reduce | flops 256 | bytes 2048 | tf_op jit(solution)/shard_map/psum | solution.py:92
  (31 shorter events, 0.6 us)
Async XLA Ops:
  7.2 2.7 copy-start
  7.2 31.5 %copy-start.3 = (bf16[8,32,640]{2,1,0:T(8,128)(2,1)S(1)}, bf16[8,32,640]{2,1,0:T(8,128)(2,1)}, u32[]{:S(2)}) copy-start(bf16[8,32,640]{2,1,0:T(8,128)(2,1)} %param.14) | copy-start | bytes 983044
  7.2 31.5 %copy-start.2 = (bf16[8,32,640]{2,1,0:T(8,128)(2,1)S(1)}, bf16[8,32,640]{2,1,0:T(8,128)(2,1)}, u32[]{:S(2)}) copy-start(bf16[8,32,640]{2,1,0:T(8,128)(2,1)} %param.15) | copy-start | bytes 983044
  7.2 103.7 %all-gather.6.cloned.1.call-start = ((), (), s32[]{:S(2)}) async-start(), calls=%async_computation.3 | async-start | bytes 7077888 | tf_op jit(solution)/shard_map/all_gather | solution.py:30
  13.3 28.3 %copy-start.5 = (bf16[5120]{0:T(1024)(128)(2,1)S(1)}, bf16[5120]{0:T(1024)(128)(2,1)}, u32[]{:S(2)}) copy-start(bf16[5120]{0:T(1024)(128)(2,1)} %param.19) | copy-start | bytes 30724
  13.3 28.3 %copy-start.6 = (s32[1,3]{1,0:T(1,128)S(1)}, s32[1,3]{1,0:T(1,128)}, u32[]{:S(2)}) copy-start(s32[1,3]{1,0:T(1,128)} %param.21) | copy-start | bytes 40
  36.1 129.7 %all-gather.4.cloned.1.call-start = ((), (), s32[]{:S(2)}) async-start(), calls=%async_computation.1 | async-start | bytes 6758400 | tf_op jit(solution)/shard_map/all_gather | solution.py:70
  36.8 190.9 %all-gather.8.cloned.1.call-start = ((), (), s32[]{:S(2)}) async-start(), calls=%async_computation.4 | async-start | bytes 6488064 | tf_op jit(solution)/shard_map/all_gather | solution.py:37
  38.6 277.4 %all-reduce.2.cloned.1.call-start = ((), (), s32[]{:S(2)}) async-start(), calls=%async_computation.2 | async-start | bytes 5242880 | tf_op jit(solution)/shard_map/psum | solution.py:73
  227.7 88.3 %copy-start.1 = (bf16[1,32,5120]{2,1,0:T(8,128)(2,1)S(1)}, bf16[1,32,5120]{2,1,0:T(8,128)(2,1)}, u32[]{:S(2)}) copy-start(bf16[1,32,5120]{2,1,0:T(8,128)(2,1)} %param.17) | copy-start | bytes 983044
  237.6 81.5 %copy-start.4 = (bf16[5120]{0:T(1024)(128)(2,1)S(1)}, bf16[5120]{0:T(1024)(128)(2,1)}, u32[]{:S(2)}) copy-start(bf16[5120]{0:T(1024)(128)(2,1)} %param.20) | copy-start | bytes 30724
Sparse Core Ops, SparseCore 0:
  36.2 74.6 all-gather.5
  113.4 52.2 all-gather.3
  168.8 58.8 all-gather.7
  229.9 86.0 all-reduce.1
where the time goes:
time: 345 us; the launch traced here: 344 us
  waiting for transfers between devices  237 us (69%)
  blocking collectives  38.1 us (11%)
  other arithmetic  20.9 us (6%)
  matrix products  19.1 us (6%)
  between operations  15.8 us (5%)
  local copies, waits for them, and re-layouts  13.1 us (4%)
    psum x1, waiting for transfers between devices, body(): lax.psum(term_rows.astype(jnp.bfloat16), 'tensor').astype(jnp.float32)  72.1 us
    all_gather x1, waiting for transfers between devices, encode(): whole_rows = lax.all_gather(rows_in, 'tensor', axis=3, tiled=True)  66.2 us
    all_gather x1, waiting for transfers between devices, body(): lax.all_gather(out_weight, 'dp', axis=1, tiled=True)  50.6 us
    all_gather x1, waiting for transfers between devices, encode(): portion = lax.all_gather(blend_weight, 'dp', axis=0, tiled=True)  47.1 us
    all_to_all x1, blocking collectives, body(): lax.all_to_all(outgoing, 'dp', split_axis=0, concat_axis=0, tiled=True)  21 us
    psum x1, blocking collectives, body(): cand_score = lax.psum(vote_sums, 'tensor')  17.1 us
    dot_general x1, matrix products, encode(): jnp.dot(blend_normed, portion.reshape(portion.shape[0], columns), preferr...  9.89 us
    convert_element_type x1, other arithmetic, encode(): (as_float * scale_rows * blend_gain.astype(jnp.float32)).astype(jnp.bfloa...  8.16 us
  transfers between devices with their start and end apart: 4, of which 4 were waited for; matrix products, arithmetic and copies ran while one was open for 12% of the time, Pallas kernels for 0%

commit v1 on v0

--- a/solution.py
+++ b/solution.py
@@ -1,3 +1,4 @@
+import functools
 import math
 import jax
 import jax.numpy as jnp
@@ -6,6 +7,26 @@
 
 HR = 40
 HDR = 128
+
+
+def unite_the_squares(matrix, dim_k):
+    n_parts = jax.lax.psum(1, axis_name="tensor")
+    history = [(it, (it + 1) % n_parts) for it in range(n_parts)]
+    near, y_new = ([matrix], [matrix])
+    buffer = [(it, (it - 1) % n_parts) for it in range(n_parts)]
+    for _ in range(n_parts // 2):
+        near.append(jax.lax.ppermute(near[-1], perm=history, axis_name="tensor"))
+    d = 0
+    while d < (n_parts - 1) // 2:
+        y_new.append(jax.lax.ppermute(y_new[-1], axis_name="tensor", perm=buffer))
+        d = d + 1
+    newest = jnp.concatenate([*near[::-1], *y_new[1:]], dim_k)
+    return jnp.roll(
+        newest, (jax.lax.axis_index("tensor") - n_parts // 2) * matrix.shape[dim_k], dim_k
+    )
+
+
+produce_surface = functools.partial(unite_the_squares, dim_k=3)
 
 
 def pair_attention(queries, keys_in, values_in, head_count):
@@ -27,7 +48,7 @@
 
 
 def encode(rows_in, blend_gain, blend_weight):
-    whole_rows = lax.all_gather(rows_in, "tensor", axis=3, tiled=True)
+    whole_rows = produce_surface(rows_in)
     prompts, pick_count, length, features = whole_rows.shape
     flat_rows = whole_rows.reshape(prompts * pick_count * length, features)
     as_float = flat_rows.astype(jnp.float32)

time: 345 us -> 266 us (0.77)
  waiting for transfers between devices: 237 us -> 124 us
  local copies, waits for them, and re-layouts: 13.1 us -> 32.4 us
  starting transfers between devices: 0.16 us -> 12.1 us
    all_gather x1 -> x0, waiting for transfers between devices: 66.2 us -> none  [encode(): whole_rows = lax.all_gather(rows_in, 'tensor', axis=3, tiled=True)]
    ppermute x0 -> x7, waiting for transfers between devices: none -> 61.5 us  [the longest x4 58.4 us: unite_the_squares(): near.append(jax.lax.ppermute(near[-1], perm=history, axis_name='tensor'))]
    all_gather x1, waiting for transfers between devices: 50.6 us -> 0.02 us  [body(): lax.all_gather(out_weight, 'dp', axis=1, tiled=True)]
    all_gather x1, waiting for transfers between devices: 47.1 us -> 0.01 us  [encode(): portion = lax.all_gather(blend_weight, 'dp', axis=0, tiled=True)]
    unnamed x16 -> x33, local copies, waits for them, and re-layouts: 4.41 us -> 22 us
    ppermute x0 -> x7, starting transfers between devices: none -> 12 us  [the longest x3 9.95 us: unite_the_squares(): y_new.append(jax.lax.ppermute(y_new[-1], axis_name='tensor', perm=buffer))]
    psum x1, waiting for transfers between devices: 72.1 us -> 62.2 us  [body(): lax.psum(term_rows.astype(jnp.bfloat16), 'tensor').astype(jnp.float32)]
  transfers between devices with their start and end apart: 4 -> 10, of which waited for: 4 -> 6; matrix products, arithmetic and copies ran while one was open for 12% -> 24% of each run, Pallas kernels for 0% -> 0%
where the time goes in v1:
time: 266 us; the launch traced here: 265 us
  waiting for transfers between devices  124 us (47%)
  blocking collectives  40.2 us (15%)
  local copies, waits for them, and re-layouts  32.4 us (12%)
  matrix products  22.2 us (8%)
  other arithmetic  18 us (7%)
  between operations  15.9 us (6%)
  starting transfers between devices  12.1 us (5%)
    psum x1, waiting for transfers between devices, body(): lax.psum(term_rows.astype(jnp.bfloat16), 'tensor').astype(jnp.float32)  62.2 us
    ppermute x4, waiting for transfers between devices, unite_the_squares(): near.append(jax.lax.ppermute(near[-1], perm=history, axis_name='tensor'))  58.4 us
    all_to_all x1, blocking collectives, body(): lax.all_to_all(outgoing, 'dp', split_axis=0, concat_axis=0, tiled=True)  23.2 us
    unnamed x33, local copies, waits for them, and re-layouts  22 us
    psum x1, blocking collectives, body(): cand_score = lax.psum(vote_sums, 'tensor')  17.1 us
    dot_general x1, matrix products, encode(): jnp.dot(blend_normed, portion.reshape(portion.shape[0], columns), preferr...  10.1 us
    ppermute x3, starting transfers between devices, unite_the_squares(): y_new.append(jax.lax.ppermute(y_new[-1], axis_name='tensor', perm=buffer))  9.95 us
    convert_element_type x1, other arithmetic, encode(): (as_float * scale_rows * blend_gain.astype(jnp.float32)).astype(jnp.bfloa...  8.13 us
  transfers between devices with their start and end apart: 10, of which 6 were waited for; matrix products, arithmetic and copies ran while one was open for 24% of the time, Pallas kernels for 0%

profile of v1, /device:TPU:2, one launch (start us, length us, event | category | flops | bytes accessed | tf_op | source)
XLA Modules:
  0.0 265.3 jit_solution(11634454347797833627)
XLA Ops:
  8.0 1.7 copy.63
  13.8 2.6 gather_fusion.1
  16.4 23.2 %all_to_all.5 = bf16[32,3,8,512]{3,2,1,0:T(8,128)(2,1)S(1)} all-to-all(bf16[32,3,8,512]{3,2,1,0:T(8,128)(2,1)} %gather_fusion.1), channel_id=1, replica_groups=mesh['dp'=32,'tensor'=8] {'dp'}, dimensions={0} | all-to-all | bytes 1572864 | tf_op jit(solution)/shard_map/all_to_all | solution.py:129
  39.5 2.0 collective-permute-start
  41.6 22.2 %collective-permute-done = bf16[32,3,8,512]{3,2,1,0:T(8,128)(2,1)S(1)} collective-permute-done((bf16[32,3,8,512]{3,2,1,0:T(8,128)(2,1)S(1)}, bf16[32,3,8,512]{3,2,1,0:T(8,128)(2,1)S(1)}, u32[]{:S(2)}, u32[]{:S(2)}) %collective-permute-start) | collective-permute-done | bytes 786464 | tf_op jit(solution)/shard_map/ppermute | solution.py:18
  63.8 3.2 %collective-permute-start.4 = (bf16[32,3,8,512]{3,2,1,0:T(8,128)(2,1)S(1)}, bf16[32,3,8,512]{3,2,1,0:T(8,128)(2,1)}, u32[]{:S(2)}, u32[]{:S(2)}) collective-permute-start(bf16[32,3,8,512]{3,2,1,0:T(8,128)(2,1)S(1)} %all_to_all.5), channel_id=1, source_target_pairs={{0,7},{1,0},{2,1},{3,2},{4,3},{5,4},{6,5},{7,6},{8,15},{9,8},{10,9... | collective-permute-start | bytes 2359304 | tf_op jit(solution)/shard_map/ppermute | solution.py:21
  67.0 16.7 %collective-permute-done.1 = bf16[32,3,8,512]{3,2,1,0:T(8,128)(2,1)S(1)} collective-permute-done((bf16[32,3,8,512]{3,2,1,0:T(8,128)(2,1)S(1)}, bf16[32,3,8,512]{3,2,1,0:T(8,128)(2,1)S(1)}, u32[]{:S(2)}, u32[]{:S(2)}) %collective-permute-start.1) | collective-permute-done | bytes 786464 | tf_op jit(solution)/shard_map/ppermute | solution.py:18
  83.7 3.2 %collective-permute-start.5 = (bf16[32,3,8,512]{3,2,1,0:T(8,128)(2,1)}, bf16[32,3,8,512]{3,2,1,0:T(8,128)(2,1)}, u32[]{:S(2)}, u32[]{:S(2)}) collective-permute-start(bf16[32,3,8,512]{3,2,1,0:T(8,128)(2,1)} %collective-permute-done.4), channel_id=1, source_target_pairs={{0,7},{1,0},{2,1},{3,2},{4,3},{5,4},{6,5},{7,6},{8,15},{9,8},{10,9... | collective-permute-start | bytes 2359304 | tf_op jit(solution)/shard_map/ppermute | solution.py:21
  86.9 15.9 %collective-permute-done.2 = bf16[32,3,8,512]{3,2,1,0:T(8,128)(2,1)} collective-permute-done((bf16[32,3,8,512]{3,2,1,0:T(8,128)(2,1)S(1)}, bf16[32,3,8,512]{3,2,1,0:T(8,128)(2,1)}, u32[]{:S(2)}, u32[]{:S(2)}) %collective-permute-start.2) | collective-permute-done | bytes 786464 | tf_op jit(solution)/shard_map/ppermute | solution.py:18
  103.5 2.0 fusion.32
  105.5 1.4 convolution_multiply_fusion
  106.9 2.1 fusion.6
  110.8 1.3 fusion.31
  114.1 3.5 %collective-permute-start.6 = (bf16[32,3,8,512]{3,2,1,0:T(8,128)(2,1)}, bf16[32,3,8,512]{3,2,1,0:T(8,128)(2,1)S(1)}, u32[]{:S(2)}, u32[]{:S(2)}) collective-permute-start(bf16[32,3,8,512]{3,2,1,0:T(8,128)(2,1)} %collective-permute-done.5), channel_id=1, source_target_pairs={{0,7},{1,0},{2,1},{3,2},{4,3},{5,4},{6,5},{7,6},{8,15},{9,8},{10,9... | collective-permute-start | bytes 2359304 | tf_op jit(solution)/shard_map/ppermute | solution.py:21
  117.6 3.6 %collective-permute-done.3 = bf16[32,3,8,512]{3,2,1,0:T(8,128)(2,1)} collective-permute-done((bf16[32,3,8,512]{3,2,1,0:T(8,128)(2,1)}, bf16[32,3,8,512]{3,2,1,0:T(8,128)(2,1)}, u32[]{:S(2)}, u32[]{:S(2)}) %collective-permute-start.3) | collective-permute-done | bytes 786464 | tf_op jit(solution)/shard_map/ppermute | solution.py:18
  122.4 1.2 constant_dynamic-update-slice_fusion.14
  123.7 1.2 constant_dynamic-update-slice_fusion.13
  124.9 1.4 constant_dynamic-update-slice_fusion.12
  126.4 1.3 constant_dynamic-update-slice_fusion.10
  128.9 3.2 %collective-permute-done.6 = bf16[32,3,8,512]{3,2,1,0:T(8,128)(2,1)S(1)} collective-permute-done((bf16[32,3,8,512]{3,2,1,0:T(8,128)(2,1)}, bf16[32,3,8,512]{3,2,1,0:T(8,128)(2,1)S(1)}, u32[]{:S(2)}, u32[]{:S(2)}) %collective-permute-start.6) | collective-permute-done | bytes 786464 | tf_op jit(solution)/shard_map/ppermute | solution.py:21
  132.1 1.4 constant_dynamic-update-slice_fusion.7
  135.1 1.2 constant_dynamic-update-slice_fusion.2
  137.7 4.6 %copy-done.1 = bf16[32,3,8,8192]{3,2,1,0:T(8,128)(2,1)} copy-done((bf16[32,3,8,8192]{3,2,1,0:T(8,128)(2,1)}, bf16[32,3,8,8192]{3,2,1,0:T(8,128)(2,1)S(1)}, u32[]{:S(2)}) %copy-start.1) | copy-done | bytes 12582936
  142.2 1.3 fusion.1
  143.8 6.6 %convolution_convert_fusion = bf16[256,5120]{1,0:T(8,128)(2,1)} fusion(bf16[640,5120]{0,1:T(8,128)(2,1)} %all-gather.3.cloned.1.call-done, bf16[32,8,5,128]{3,2,1,0:T(8,128)(2,1)S(1)} %bitcast.74), kind=kOutput, calls=%fused_computation.8 | convolution fusion | flops 1679032320 | bytes 9502720 | tf_op jit(solution)/shard_map/dot_general | solution.py:89
  150.4 8.1 %fusion.3 = bf16[32,3,8,4096]{3,2,1,0:T(8,128)(2,1)} fusion(f32[4096]{0:T(1024)S(1)} %convert_element_type.58, f32[32,3,8]{2,1,0:T(4,128)S(1)} %copy.62, bf16[32,3,8,8192]{3,2,1,0:T(8,128)(2,1)} %copy-done.1, s32[]{:T(128)S(6)} %select_n.76), kind=kLoop, calls=%fused_computation.7 | loop fusion | flops 12582912 | bytes 12602372 | tf_op jit(solution)/shard_map/convert_element_type | solution.py:56
  158.6 10.1 %convolution_convert_fusion.1 = bf16[768,768]{1,0:T(8,128)(2,1)} fusion(bf16[768,4096]{1,0:T(8,128)(2,1)} %bitcast.72, bf16[4096,768]{0,1:T(8,128)(2,1)} %bitcast.76), kind=kOutput, calls=%fused_computation.9 | convolution fusion | flops 4832428032 | bytes 13762560 | tf_op jit(solution)/shard_map/dot_general | solution.py:59
  168.7 3.7 %reshape.140 = bf16[32,24,3,256]{3,2,1,0:T(4,128)(2,1)} reshape(bf16[768,768]{1,0:T(8,128)(2,1)} %convolution_convert_fusion.1) | data formatting | bytes 2359296 | tf_op jit(solution)/shard_map/reshape | solution.py:62
  172.4 2.6 copy.64
  175.0 62.2 %all-reduce.2.cloned.1.call-done = bf16[256,5120]{1,0:T(8,128)(2,1)} async-done(((bf16[256,5120]{1,0:T(8,128)(2,1)}), bf16[256,5120]{1,0:T(8,128)(2,1)}) %all-reduce.2.cloned.1.call-update) | async-done | bytes 2621456 | tf_op jit(solution)/shard_map/psum | solution.py:94
  238.4 1.8 fusion.7
  241.7 17.1 %psum.15 = f32[32,8]{0,1:T(8,128)} all-reduce(f32[32,8]{0,1:T(8,128)S(1)} %select_subtract_fusion), channel_id=1, replica_groups=mesh['dp'=32,'tensor'=8] {'tensor'}, use_global_device_ids=true, to_apply=%region_5.6 | all-reduce | flops 256 | bytes 2048 | tf_op jit(solution)/shard_map/psum | solution.py:113
  (60 shorter events, 15.7 us)
Async XLA Ops:
  7.2 3.6 %copy-start = (bf16[32,8,8,512]{3,2,1,0:T(8,128)(2,1)S(1)}, bf16[32,8,8,512]{3,2,1,0:T(8,128)(2,1)}, u32[]{:S(2)}) copy-start(bf16[32,8,8,512]{3,2,1,0:T(8,128)(2,1)} %param.25) | copy-start | bytes 6291460
  7.2 136.6 %all-gather.3.cloned.1.call-start = ((), (), s32[]{:S(2)}) async-start(), calls=%async_computation.1 | async-start | bytes 6758400 | tf_op jit(solution)/shard_map/all_gather | solution.py:91
  7.9 150.7 %all-gather.5.cloned.1.call-start = ((), (), s32[]{:S(2)}) async-start(), calls=%async_computation.3 | async-start | bytes 6488064 | tf_op jit(solution)/shard_map/all_gather | solution.py:58
  9.7 227.5 %all-reduce.2.cloned.1.call-start = ((), (), s32[]{:S(2)}) async-start(), calls=%async_computation.2 | async-start | bytes 5242880 | tf_op jit(solution)/shard_map/psum | solution.py:94
  39.5 24.2 %collective-permute-start = (bf16[32,3,8,512]{3,2,1,0:T(8,128)(2,1)S(1)}, bf16[32,3,8,512]{3,2,1,0:T(8,128)(2,1)S(1)}, u32[]{:S(2)}, u32[]{:S(2)}) collective-permute-start(bf16[32,3,8,512]{3,2,1,0:T(8,128)(2,1)S(1)} %all_to_all.5), channel_id=1, source_target_pairs={{0,1},{1,2},{2,3},{3,4},{4,5},{5,6},{6,7},{7,0},{8,9},{9,10},{10,1... | collective-permute-start | bytes 2359304 | tf_op jit(solution)/shard_map/ppermute | solution.py:18
  63.8 19.9 %copy-start.2 = (bf16[32,3,8,512]{3,2,1,0:T(8,128)(2,1)}, bf16[32,3,8,512]{3,2,1,0:T(8,128)(2,1)S(1)}, u32[]{:S(2)}) copy-start(bf16[32,3,8,512]{3,2,1,0:T(8,128)(2,1)S(1)} %collective-permute-done) | copy-start | bytes 2359300
  63.8 19.9 %collective-permute-start.1 = (bf16[32,3,8,512]{3,2,1,0:T(8,128)(2,1)S(1)}, bf16[32,3,8,512]{3,2,1,0:T(8,128)(2,1)S(1)}, u32[]{:S(2)}, u32[]{:S(2)}) collective-permute-start(bf16[32,3,8,512]{3,2,1,0:T(8,128)(2,1)S(1)} %collective-permute-done), channel_id=1, source_target_pairs={{0,1},{1,2},{2,3},{3,4},{4,5},{5,6},{6,7},{7,0},{8,9},{9,10},{10,1... | collective-permute-start | bytes 2359304 | tf_op jit(solution)/shard_map/ppermute | solution.py:18
  63.8 19.9 %collective-permute-start.4 = (bf16[32,3,8,512]{3,2,1,0:T(8,128)(2,1)S(1)}, bf16[32,3,8,512]{3,2,1,0:T(8,128)(2,1)}, u32[]{:S(2)}, u32[]{:S(2)}) collective-permute-start(bf16[32,3,8,512]{3,2,1,0:T(8,128)(2,1)S(1)} %all_to_all.5), channel_id=1, source_target_pairs={{0,7},{1,0},{2,1},{3,2},{4,3},{5,4},{6,5},{7,6},{8,15},{9,8},{10,9... | collective-permute-start | bytes 2359304 | tf_op jit(solution)/shard_map/ppermute | solution.py:21
  83.7 3.2 %copy-start.4 = (bf16[32,3,8,512]{3,2,1,0:T(8,128)(2,1)}, bf16[32,3,8,512]{3,2,1,0:T(8,128)(2,1)S(1)}, u32[]{:S(2)}) copy-start(bf16[32,3,8,512]{3,2,1,0:T(8,128)(2,1)S(1)} %collective-permute-done.1) | copy-start | bytes 2359300
  83.7 19.1 %collective-permute-start.2 = (bf16[32,3,8,512]{3,2,1,0:T(8,128)(2,1)S(1)}, bf16[32,3,8,512]{3,2,1,0:T(8,128)(2,1)}, u32[]{:S(2)}, u32[]{:S(2)}) collective-permute-start(bf16[32,3,8,512]{3,2,1,0:T(8,128)(2,1)S(1)} %collective-permute-done.1), channel_id=1, source_target_pairs={{0,1},{1,2},{2,3},{3,4},{4,5},{5,6},{6,7},{7,0},{8,9},{9,10},{10,1... | collective-permute-start | bytes 2359304 | tf_op jit(solution)/shard_map/ppermute | solution.py:18
  83.7 30.4 %collective-permute-start.5 = (bf16[32,3,8,512]{3,2,1,0:T(8,128)(2,1)}, bf16[32,3,8,512]{3,2,1,0:T(8,128)(2,1)}, u32[]{:S(2)}, u32[]{:S(2)}) collective-permute-start(bf16[32,3,8,512]{3,2,1,0:T(8,128)(2,1)} %collective-permute-done.4), channel_id=1, source_target_pairs={{0,7},{1,0},{2,1},{3,2},{4,3},{5,4},{6,5},{7,6},{8,15},{9,8},{10,9... | collective-permute-start | bytes 2359304 | tf_op jit(solution)/shard_map/ppermute | solution.py:21
  102.8 18.4 %collective-permute-start.3 = (bf16[32,3,8,512]{3,2,1,0:T(8,128)(2,1)}, bf16[32,3,8,512]{3,2,1,0:T(8,128)(2,1)}, u32[]{:S(2)}, u32[]{:S(2)}) collective-permute-start(bf16[32,3,8,512]{3,2,1,0:T(8,128)(2,1)} %collective-permute-done.2), channel_id=1, source_target_pairs={{0,1},{1,2},{2,3},{3,4},{4,5},{5,6},{6,7},{7,0},{8,9},{9,10},{10,1... | collective-permute-start | bytes 2359304 | tf_op jit(solution)/shard_map/ppermute | solution.py:18
  114.1 20.7 %copy-start.5 = (bf16[32,3,8,512]{3,2,1,0:T(8,128)(2,1)S(1)}, bf16[32,3,8,512]{3,2,1,0:T(8,128)(2,1)}, u32[]{:S(2)}) copy-start(bf16[32,3,8,512]{3,2,1,0:T(8,128)(2,1)} %copy-done.4) | copy-start | bytes 2359300
  114.1 20.8 %copy-start.3 = (bf16[32,3,8,512]{3,2,1,0:T(8,128)(2,1)S(1)}, bf16[32,3,8,512]{3,2,1,0:T(8,128)(2,1)}, u32[]{:S(2)}) copy-start(bf16[32,3,8,512]{3,2,1,0:T(8,128)(2,1)} %copy-done.2) | copy-start | bytes 2359300
  114.1 17.9 %collective-permute-start.6 = (bf16[32,3,8,512]{3,2,1,0:T(8,128)(2,1)}, bf16[32,3,8,512]{3,2,1,0:T(8,128)(2,1)S(1)}, u32[]{:S(2)}, u32[]{:S(2)}) collective-permute-start(bf16[32,3,8,512]{3,2,1,0:T(8,128)(2,1)} %collective-permute-done.5), channel_id=1, source_target_pairs={{0,7},{1,0},{2,1},{3,2},{4,3},{5,4},{6,5},{7,6},{8,15},{9,8},{10,9... | collective-permute-start | bytes 2359304 | tf_op jit(solution)/shard_map/ppermute | solution.py:21
  137.7 4.6 %copy-start.1 = (bf16[32,3,8,8192]{3,2,1,0:T(8,128)(2,1)}, bf16[32,3,8,8192]{3,2,1,0:T(8,128)(2,1)S(1)}, u32[]{:S(2)}) copy-start(bf16[32,3,8,8192]{3,2,1,0:T(8,128)(2,1)S(1)} %constant_dynamic-update-slice_fusion) | copy-start | bytes 37748740
  158.6 78.6 %copy-start.6 = (bf16[1,32,5120]{2,1,0:T(8,128)(2,1)S(1)}, bf16[1,32,5120]{2,1,0:T(8,128)(2,1)}, u32[]{:S(2)}) copy-start(bf16[1,32,5120]{2,1,0:T(8,128)(2,1)} %param.17) | copy-start | bytes 983044
  158.6 81.7 %copy-start.7 = (bf16[5120]{0:T(1024)(128)(2,1)S(1)}, bf16[5120]{0:T(1024)(128)(2,1)}, u32[]{:S(2)}) copy-start(bf16[5120]{0:T(1024)(128)(2,1)} %param.20) | copy-start | bytes 30724
Sparse Core Ops, SparseCore 0:
  10.6 61.8 all-gather.2
  74.9 58.8 all-gather.4
  150.6 86.6 all-reduce.1
